TPU v7x, 32 devices: a whole 2x2x4 slice. The times are simulated.
32 devices in a mesh: grp: 2 (over y), ctx: 4 (over z), head: 4 (over x, core).
Axes of the slice: x: 2, y: 2, z: 4, core: 2. Of those that a mesh axis runs over, the one named last changes fastest.
Arguments:
- queries: bfloat16 [1024, 8192], P(('grp', 'ctx'), 'head'), parts along dimension 0, may hold values from -5 to 5
- keys: bfloat16 [1024, 1024], P(('grp', 'ctx'), 'head'), parts along dimension 0, may hold values from -5 to 5
- values: bfloat16 [1024, 1024], P(('grp', 'ctx'), 'head'), parts along dimension 0, may hold values from -6 to 6
- d_out: bfloat16 [1024, 8192], P(('grp', 'ctx'), 'head'), parts along dimension 0, may hold values from -6 to 6
- span_order: int32 [4], replicated, may hold values from 0 to 3, each once
- pattern: int32 [4, 2], replicated, may hold values from 0 to 3, as said below
Outputs:
- d_queries: bfloat16 [1024, 8192], P(('grp', 'ctx'), 'head'), parts along dimension 0
- key_gradients: bfloat16 [1024, 1024], P(('grp', 'ctx'), 'head'), parts along dimension 0
- value_gradients: bfloat16 [1024, 1024], P(('grp', 'ctx'), 'head'), parts along dimension 0
There are 2 independent parts, one for each index of `grp`. A program takes and returns all parts, laid end to end along the dimension named above; an argument that names none is the same for every part. Nothing has to cross between parts.
Inputs may be any that keep to these rules, and one draw needn't show every extreme that they name: `span_order`: a permutation of the 4 block positions. `pattern`: each row names 2 distinct blocks, its own block first.
All inputs are finite; a program needn't handle non-finite values.
Results may differ from a plain program's by a relative error of at most 0.0075.
Values may be sent and summed in bfloat16 or wider, within the bound.
No kernel may reach another device: no remote copies, remote signals or barrier semaphores. Data moves between devices by JAX's collectives and lax.ppermute only.
A program may use at most 64 MiB of HBM per device.

v0:
```python
import math
import jax
import jax.numpy as jnp
from jax import lax
from jax.sharding import PartitionSpec as P

QUERY_HEADS = 64
KEY_VALUE_HEADS = 8
HEAD_SIZE = 128
BLOCK = 128
NEG = -1e30


def heads_first(dense_matrix, key_value_count):
    return dense_matrix.reshape(
        dense_matrix.shape[0], key_value_count, QUERY_HEADS // KEY_VALUE_HEADS, HEAD_SIZE
    ).transpose(1, 2, 0, 3)


def key_mask(start, count, local_pattern, query_pos, span_order):
    key_blocks = start // BLOCK + jnp.arange(count // BLOCK, dtype=jnp.int32)
    named = jnp.any(local_pattern[:, :, None] == key_blocks[None, None, :], axis=1)
    local_blocks = local_pattern.shape[0]
    named_rows = jnp.broadcast_to(
        named[:, None, :, None], (local_blocks, BLOCK, count // BLOCK, BLOCK)
    )
    named_rows = named_rows.reshape(local_blocks * BLOCK, count)
    key_order = lax.dynamic_slice_in_dim(span_order, start // BLOCK, count // BLOCK, 0)
    key_pos = (key_order[:, None] * BLOCK + jnp.arange(BLOCK, dtype=jnp.int32)[None, :]).reshape(
        count
    )
    return named_rows & (key_pos[None, :] <= query_pos[:, None])


def sweep(step, carry, key_piece, value_piece, start):
    count = key_piece.shape[0]
    width = BLOCK * math.gcd(count // BLOCK, max(1, 512 // BLOCK))
    turns = count // width
    if turns == 1:
        return step(carry, key_piece, value_piece, start)

    def advance(index, inner):
        offset = index * width
        key_part = lax.dynamic_slice_in_dim(key_piece, offset, width, 0)
        value_part = lax.dynamic_slice_in_dim(value_piece, offset, width, 0)
        return step(inner, key_part, value_part, start + offset)

    return lax.fori_loop(0, turns, advance, carry)


def on_device(queries, keys, values, d_out, span_order, pattern):
    rows = queries.shape[0]
    key_value_count = keys.shape[1] // HEAD_SIZE
    query_group = QUERY_HEADS // KEY_VALUE_HEADS
    blocks_here = rows // BLOCK
    scale = 1.0 / math.sqrt(HEAD_SIZE)
    first_block = lax.axis_index("ctx") * blocks_here
    local_pattern = lax.dynamic_slice_in_dim(pattern, first_block, blocks_here, 0)
    local_order = lax.dynamic_slice_in_dim(span_order, first_block, blocks_here, 0)
    query_pos = (
        local_order[:, None] * BLOCK + jnp.arange(BLOCK, dtype=jnp.int32)[None, :]
    ).reshape(rows)
    query_heads = heads_first(queries, key_value_count)
    grad_heads = heads_first(d_out, key_value_count)
    total_rows = rows * lax.axis_size("ctx")

    def scores_for(key_piece):
        key_heads = key_piece.reshape(key_piece.shape[0], key_value_count, HEAD_SIZE)
        return (
            jnp.einsum("kgtd,rkd->kgtr", query_heads, key_heads, preferred_element_type=jnp.float32)
            * scale
        )

    def forward_step(carry, key_piece, value_piece, start):
        allowed = key_mask(start, key_piece.shape[0], local_pattern, query_pos, span_order)

        def forward_update(state):
            running_max, total, weighted = state
            scores = scores_for(key_piece)
            new_max = jnp.maximum(running_max, jnp.max(jnp.where(allowed, scores, NEG), axis=-1))
            factor = jnp.exp(running_max - new_max)
            weights = jnp.where(allowed, jnp.exp(scores - new_max[..., None]), 0.0)
            value_heads = value_piece.reshape(
                value_piece.shape[0], key_value_count, HEAD_SIZE
            ).astype(jnp.float32)
            product = jnp.einsum(
                "kgtr,rkd->kgtd", weights, value_heads, precision=lax.Precision.HIGHEST
            )
            return (
                new_max,
                total * factor + jnp.sum(weights, axis=-1),
                weighted * factor[..., None] + product,
            )

        return lax.cond(jnp.any(allowed), forward_update, lambda state: state, carry)

    def make_backward(log_total, delta, anchor):

        def step(carry, key_piece, value_piece, start):
            count = key_piece.shape[0]
            allowed = key_mask(start, count, local_pattern, query_pos, span_order)

            def step_update(state):
                query_grad, key_grads = state
                key_heads = key_piece.reshape(count, key_value_count, HEAD_SIZE)
                value_heads = value_piece.reshape(count, key_value_count, HEAD_SIZE)
                scores = scores_for(key_piece)
                probs = jnp.where(allowed, jnp.exp(scores - log_total[..., None]), 0.0)
                grad_probs = jnp.einsum(
                    "kgtd,rkd->kgtr", grad_heads, value_heads, preferred_element_type=jnp.float32
                )
                grad_scores = (probs * (grad_probs - delta[..., None])).astype(jnp.bfloat16)
                query_grad = query_grad + jnp.einsum(
                    "kgtr,rkd->kgtd", grad_scores, key_heads, preferred_element_type=jnp.float32
                )
                key_part = (
                    jnp.einsum(
                        "kgtr,kgtd->rkd",
                        grad_scores,
                        query_heads,
                        preferred_element_type=jnp.float32,
                    )
                    * scale
                )
                value_part = jnp.einsum(
                    "kgtr,kgtd->rkd",
                    probs.astype(jnp.bfloat16),
                    grad_heads,
                    preferred_element_type=jnp.float32,
                )
                joined = jnp.stack(
                    (
                        key_part.reshape(count, key_value_count * HEAD_SIZE),
                        value_part.reshape(count, key_value_count * HEAD_SIZE),
                    ),
                    axis=1,
                )
                offset = start - anchor
                former = lax.dynamic_slice_in_dim(key_grads, offset, count, 0)
                key_grads = lax.dynamic_update_slice_in_dim(key_grads, former + joined, offset, 0)
                return (query_grad, key_grads)

            return lax.cond(jnp.any(allowed), step_update, lambda state: state, carry)

        return step

    start_state = (
        jnp.full((key_value_count, query_group, rows), NEG, jnp.float32),
        jnp.zeros((key_value_count, query_group, rows), jnp.float32),
        jnp.zeros((key_value_count, query_group, rows, HEAD_SIZE), jnp.float32),
    )
    query_zero = jnp.zeros((key_value_count, query_group, rows, HEAD_SIZE), jnp.float32)
    state = sweep(
        forward_step,
        start_state,
        lax.all_gather(keys, "ctx", axis=0, tiled=True),
        lax.all_gather(values, "ctx", axis=0, tiled=True),
        jnp.int32(0),
    )
    running_max, total, weighted = state
    attended = weighted / total[..., None]
    log_total = running_max + jnp.log(total)
    delta = jnp.sum(grad_heads * attended, axis=-1)
    log_total, delta = (log_total, delta)
    both_step = make_backward(log_total, delta, 0)
    grad_zero = jnp.zeros((total_rows, 2, key_value_count * HEAD_SIZE), jnp.float32)
    query_grad, key_grads = sweep(
        both_step,
        (query_zero, grad_zero),
        lax.all_gather(keys, "ctx", axis=0, tiled=True),
        lax.all_gather(values, "ctx", axis=0, tiled=True),
        jnp.int32(0),
    )
    summed = lax.psum_scatter(key_grads, "ctx", scatter_dimension=0, tiled=True)
    d_queries = (
        (query_grad * scale)
        .transpose(2, 0, 1, 3)
        .reshape(rows, key_value_count * query_group * HEAD_SIZE)
        .astype(jnp.bfloat16)
    )
    key_gradients = summed[:, 0, :].astype(jnp.bfloat16)
    value_gradients = summed[:, 1, :].astype(jnp.bfloat16)
    return (d_queries, key_gradients, value_gradients)


def solution(mesh):
    return jax.shard_map(
        on_device,
        mesh=mesh,
        in_specs=(
            P(("grp", "ctx"), "head"),
            P(("grp", "ctx"), "head"),
            P(("grp", "ctx"), "head"),
            P(("grp", "ctx"), "head"),
            P(),
            P(),
        ),
        out_specs=(P(("grp", "ctx"), "head"), P(("grp", "ctx"), "head"), P(("grp", "ctx"), "head")),
        check_vma=False,
    )
```

profile of v0, /device:TPU:0, one launch (start us, length us, event | category | flops | bytes accessed | tf_op | source)
XLA Modules:
  0.0 102.2 jit_solution(14186769745617313074)
XLA Ops:
  7.2 0.7 broadcast_multiply_fusion
  7.9 1.2 %dynamic_slice.12 = s32[1]{0:T(128)} dynamic-slice(s32[4]{0:T(128)} %param.14, s32[]{:T(128)S(6)} %select_n.23), dynamic_slice_sizes={1} | dynamic-slice | bytes 12 | tf_op jit(solution)/shard_map/dynamic_slice | solution.py:59
  10.2 0.8 and_reduce_fusion
  11.7 15.8 %all_gather.8 = bf16[512,256]{1,0:T(8,128)(2,1)S(1)} all-gather(bf16[128,256]{1,0:T(8,128)(2,1)} %param.11), channel_id=1, replica_groups=mesh['grp'=2,'ctx'=4,'head'=4] {'ctx'}, dimensions={0}, use_global_device_ids=true | all-gather | bytes 327680 | tf_op jit(solution)/shard_map/all_gather | solution.py:170
  27.5 14.8 %all_gather.9 = bf16[512,256]{1,0:T(8,128)(2,1)S(1)} all-gather(bf16[128,256]{1,0:T(8,128)(2,1)} %param.12), channel_id=1, replica_groups=mesh['grp'=2,'ctx'=4,'head'=4] {'ctx'}, dimensions={0}, use_global_device_ids=true | all-gather | bytes 327680 | tf_op jit(solution)/shard_map/all_gather | solution.py:171
  42.3 1.3 %copy.29 = bf16[128,2048]{0,1:T(8,128)(2,1)S(1)} copy(bf16[128,2048]{1,0:T(8,128)(2,1)} %param.10) | data formatting | bytes 1048576 | tf_op args[0]
  43.6 1.3 %copy.31 = bf16[128,2048]{0,1:T(8,128)(2,1)S(1)} copy(bf16[128,2048]{1,0:T(8,128)(2,1)} %param.13) | data formatting | bytes 1048576 | tf_op args[3]
  45.0 0.8 copy-done.1
  45.8 0.3 copy.32
  46.3 8.0 %conditional.2 = (f32[2,8,128]{2,1,0:T(8,128)}, f32[2,8,128]{2,1,0:T(8,128)S(1)}, f32[2,8,128,128]{3,2,1,0:T(8,128)S(1)}, f32[2,8,128]{2,1,0:T(8,128)S(1)}) conditional(s32[]{:T(128)} %convert_element_type.33, () %tuple.32, (pred[128,512]{1,0:T(8,128)(4,1)S(1)}, bf16[512,256]{1,0:T(8,128)(2,1)S(1)}, bf16[2,8,128,128]{2,3,1,0:T(8,128)(2,1)S(1)}, ...), branch_computations={%region_2.3_spmd, %region_3.6_spmd} | conditional | flops 1889804288 | bytes 16023584 | solution.py:95
  46.5 1.0 select_reduce_fusion
  47.5 0.6 exponential_multiply_fusion
  48.1 2.0 %fusion.1 = f32[2,8,128]{2,1,0:T(8,128)S(1)} fusion(f32[2,8,128,512]{3,2,1,0:T(8,128)S(1)} %get-tuple-element.97, f32[2,8,128]{2,1,0:T(8,128)} %get-tuple-element.106, pred[128,512]{1,0:T(8,128)(4,1)S(1)} %get-tuple-element.55), kind=kLoop, calls=%fused_computation.3 | loop fusion | flops 4192256 | bytes 4276224 | tf_op jit(solution)/shard_map/cond/branch_1_fun/reduce_sum | solution.py:91
  50.0 3.5 %fusion.6 = f32[2,8,128,128]{3,2,1,0:T(8,128)S(1)} fusion(f32[2,8,128,512]{3,2,1,0:T(8,128)S(1)} %get-tuple-element.97, f32[2,8,128]{2,1,0:T(8,128)} %get-tuple-element.106, pred[128,512]{1,0:T(8,128)(4,1)S(1)} %get-tuple-element.55, f32[2,8,128]{2,1,0:T(8,128)S(1)} %get-tuple-element.94, bf16[512,2,128,1]{2,1,0,3:T(2,128)(2,1)S(1)} %bitcast.59), kind=kOutput, calls=%fused_computation.8 | convolution fusion | flops 1614020608 | bytes 5586944 | tf_op jit(solution)/shard_map/cond/branch_1_fun/kgtr,rkd->kgtd/dot_general | solution.py:86
  53.5 0.7 fusion.27
  54.3 8.6 %conditional.3 = (f32[2,8,128,128]{3,2,1,0:T(8,128)}, f32[512,2,256]{0,2,1:T(8,128)}) conditional(s32[]{:T(128)} %convert_element_type.33, () %tuple.31, (pred[128,512]{1,0:T(8,128)(4,1)S(1)}, bf16[512,256]{1,0:T(8,128)(2,1)S(1)}, bf16[2,8,128,128]{2,3,1,0:T(8,128)(2,1)S(1)}, f32[2,8,128]{2,1,0:T(8,128)}, f32[2,8,128]{2,1,0:T(8,128)S(1)}, ...), branch_computations={%region_6.7_spmd, %region_7.9_spmd} | conditional | flops 1353842688 | bytes 31391788 | solution.py:143
  54.3 0.7 add.60
  55.1 0.6 multiply_reduce_fusion
  55.8 0.8 fusion.21
  56.5 0.2 copy-done.2
  56.7 1.1 %fusion.14 = f32[2,512,128,1]{1,2,3,0:T(8,128)S(1)} fusion(bf16[2,8,128,128]{2,3,1,0:T(8,128)(2,1)S(1)} %copy-done.2, f32[2,8,128,512]{3,2,1,0:T(8,128)S(1)} %fusion.21, f32[2,8,128]{2,1,0:T(8,128)S(1)} %add.60, pred[128,512]{1,0:T(8,128)(4,1)S(1)} %get-tuple-element.59), kind=kOutput, calls=%fused_computation.20 | convolution fusion | flops 272629760 | bytes 5316608 | tf_op jit(solution)/shard_map/cond/branch_1_fun/kgtr,kgtd->rkd/dot_general | solution.py:125
  57.8 1.8 %multiply_convert_fusion = bf16[2,8,128,512]{3,2,1,0:T(8,128)(2,1)S(1)} fusion(f32[2,8,128,512]{3,2,1,0:T(8,128)S(1)} %fusion.21, bf16[2,8,128,128]{2,3,1,0:T(8,128)(2,1)S(1)} %copy-done.2, f32[2,8,128]{2,1,0:T(8,128)S(1)} %multiply_reduce_fusion, f32[2,8,128]{2,1,0:T(8,128)S(1)} %add.60, pred[128,512]{1,0:T(8,128)(4,1)S(1)} %get-tuple-element.59, ...), kind=kOutput, calls=%fused_computation.17 | convolution fusion | flops 274726912 | bytes 7159808 | tf_op jit(solution)/shard_map/cond/branch_1_fun/kgtd,rkd->kgtr/dot_general | solution.py:109
  59.6 0.5 fusion.17
  60.1 1.7 %fusion.19 = f32[2,8,128,128]{3,2,1,0:T(8,128)} fusion(bf16[2,8,128,512]{3,2,1,0:T(8,128)(2,1)S(1)} %multiply_convert_fusion, bf16[512,2,128,1]{2,1,0,3:T(2,128)(2,1)S(1)} %bitcast.51), kind=kOutput, calls=%fused_computation.27 | convolution fusion | flops 268435456 | bytes 3407872 | tf_op jit(solution)/shard_map/cond/branch_1_fun/kgtr,rkd->kgtd/dot_general | solution.py:113
  61.8 1.1 %pad_maximum_fusion = f32[512,2,256]{0,2,1:T(8,128)} fusion(f32[512,1,256]{0,2,1:T(8,128)S(1)} %bitcast.58, f32[512,1,256]{0,2,1:T(8,128)S(1)} %bitcast.55), kind=kLoop, calls=%fused_computation.24 | loop fusion | flops 262144 | bytes 2097152 | tf_op jit(solution)/shard_map/cond/branch_1_fun/stack | solution.py:131
  62.9 2.5 %copy.34 = f32[512,2,256]{2,0,1:T(8,128)} copy(f32[512,2,256]{0,2,1:T(8,128)} %get-tuple-element.83) | data formatting | bytes 2097152 | tf_op jit(solution)/shard_map/cond | solution.py:143
  65.5 1.4 %fusion.25 = bf16[128,2,8,128]{3,0,2,1:T(8,128)(2,1)S(1)} fusion(f32[2,8,128,128]{3,2,1,0:T(8,128)} %get-tuple-element.82), kind=kLoop, calls=%fused_computation.34 | loop fusion | flops 524288 | bytes 1572864 | tf_op jit(solution)/shard_map/convert_element_type | solution.py:179
  66.8 0.3 copy.33
  67.2 0.9 copy.69
  68.1 25.6 %reduce-scatter.2.cloned.1.call-done = f32[128,2,256]{2,0,1:T(8,128)} async-done(((f32[512,2,256]{2,0,1:T(8,128)}), f32[128,2,256]{2,0,1:T(8,128)}) %reduce-scatter.2.cloned.1.call-update) | async-done | bytes 262160 | tf_op jit(solution)/shard_map/reduce_scatter | solution.py:174
  93.7 1.0 convert.4
  94.7 0.7 slice_bitcast_fusion
  (17 shorter events, 1.0 us)
Async XLA Ops:
  7.2 2.6 %copy-start = (s32[4,2]{0,1:T(2,128)S(1)}, s32[4,2]{0,1:T(2,128)}, u32[]{:S(2)}) copy-start(s32[4,2]{0,1:T(2,128)} %param.15) | copy-start | bytes 100
  7.2 86.5 %reduce-scatter.2.cloned.1.call-start = ((), (), s32[]{:S(2)}) async-start(), calls=%async_computation.1 | async-start | bytes 1310720 | tf_op jit(solution)/shard_map/reduce_scatter | solution.py:174
  45.0 0.8 copy-start.1
  55.7 1.0 %copy-start.2 = (bf16[2,8,128,128]{2,3,1,0:T(8,128)(2,1)S(1)}, bf16[2,8,128,128]{2,3,1,0:T(8,128)(2,1)}, u32[]{:S(2)}) copy-start(bf16[2,8,128,128]{2,3,1,0:T(8,128)(2,1)} %get-tuple-element.64) | copy-start | bytes 1572868 | tf_op jit(solution)/shard_map/cond
Sparse Core Ops, SparseCore 0:
  65.6 28.0 reduce-scatter.1
where the time goes:
time: 103 us; the launch traced here: 102 us
  blocking collectives  30.7 us (30%)
  waiting for transfers between devices  25.6 us (25%)
  between operations  15.4 us (15%)
  matrix products  10.3 us (10%)
  local copies, waits for them, and re-layouts  10.2 us (10%)
  other arithmetic  9.81 us (10%)
    reduce_scatter x1, waiting for transfers between devices, on_device(): summed = lax.psum_scatter(key_grads, 'ctx', scatter_dimension=0, tiled=True)  25.6 us
    all_gather x1, blocking collectives, on_device(): lax.all_gather(keys, 'ctx', axis=0, tiled=True)  15.8 us
    all_gather x1, blocking collectives, on_device(): lax.all_gather(values, 'ctx', axis=0, tiled=True)  14.8 us
    unnamed x7, local copies, waits for them, and re-layouts  4.36 us
    dot_general x1, matrix products, forward_update(): jnp.einsum('kgtr,rkd->kgtd', weights, value_heads, precision=lax.Precisio...  3.49 us
    cond x1, local copies, waits for them, and re-layouts, step(): return lax.cond(jnp.any(allowed), step_update, lambda state: state, carry)  2.55 us
  transfers between devices with their start and end apart: 1, of which 1 were waited for; matrix products, arithmetic and copies ran while one was open for 3% of the time, Pallas kernels for 0%

commit v1 on v0

--- a/solution.py
+++ b/solution.py
@@ -1,3 +1,4 @@
+import functools
 import math
 import jax
 import jax.numpy as jnp
@@ -9,6 +10,28 @@
 HEAD_SIZE = 128
 BLOCK = 128
 NEG = -1e30
+
+
+def _reach_numbers(load, net_axis):
+    w2, x_new, back = (lax.axis_size(net_axis), lax.axis_index(net_axis), load.shape[0])
+    so_far_all = list(map(lambda c: (c, (c + 1) % w2), range(w2)))
+    gallery = list(map(lambda c: (c, (c - 1) % w2), range(w2)))
+    g_now = jnp.zeros((*load.shape[:0], w2 * back, *load.shape[1:]), load.dtype)
+    g_now = lax.dynamic_update_slice_in_dim(g_now, load, x_new * back, axis=0)
+    z_new = w2 // 2
+    rr = 1
+    val = u_next = load
+    while rr < z_new + 1:
+        val = lax.ppermute(val, net_axis, so_far_all)
+        g_now = lax.dynamic_update_slice_in_dim(g_now, val, (x_new - rr) % w2 * back, axis=0)
+        if rr < w2 - z_new:
+            u_next = lax.ppermute(u_next, net_axis, gallery)
+            g_now = lax.dynamic_update_slice_in_dim(g_now, u_next, (x_new + rr) % w2 * back, axis=0)
+        rr = rr + 1
+    return g_now
+
+
+entries_apply = functools.partial(_reach_numbers, net_axis="ctx")
 
 
 def heads_first(dense_matrix, key_value_count):
@@ -167,7 +190,7 @@
     query_grad, key_grads = sweep(
         both_step,
         (query_zero, grad_zero),
-        lax.all_gather(keys, "ctx", axis=0, tiled=True),
+        entries_apply(keys),
         lax.all_gather(values, "ctx", axis=0, tiled=True),
         jnp.int32(0),
     )

time: 103 us -> 115 us (1.12)
  starting transfers between devices: 0.04 us -> 7.59 us
  local copies, waits for them, and re-layouts: 10.2 us -> 16.1 us
  other arithmetic: 9.81 us -> 11.8 us
  waiting for transfers between devices: 25.6 us -> 23.7 us
  blocking collectives: 30.7 us -> 29.2 us
    ppermute x0 -> x3, starting transfers between devices: none -> 7.55 us  [the longest x1 5.05 us: _reach_numbers(): u_next = lax.ppermute(u_next, net_axis, gallery)]
    dynamic_update_slice x0 -> x4, local copies, waits for them, and re-layouts: none -> 2.62 us  [the longest x2 1.73 us: _reach_numbers(): lax.dynamic_update_slice_in_dim(g_now, val, (x_new - rr) % w2 * back, axi...]
    reduce_scatter x1, waiting for transfers between devices: 25.6 us -> 23.7 us  [on_device(): summed = lax.psum_scatter(key_grads, 'ctx', scatter_dimension=0, tiled=True)]
    unnamed x7 -> x10, local copies, waits for them, and re-layouts: 4.36 us -> 5.18 us
  transfers between devices with their start and end apart: 1 -> 4, of which waited for: 1 -> 1; matrix products, arithmetic and copies ran while one was open for 3% -> 18% of each run, Pallas kernels for 0% -> 0%
where the time goes in v1:
time: 115 us; the launch traced here: 114 us
  blocking collectives  29.2 us (25%)
  waiting for transfers between devices  23.7 us (21%)
  local copies, waits for them, and re-layouts  16.1 us (14%)
  between operations  15.4 us (13%)
  other arithmetic  11.8 us (10%)
  matrix products  10.4 us (9%)
  starting transfers between devices  7.59 us (7%)
    reduce_scatter x1, waiting for transfers between devices, on_device(): summed = lax.psum_scatter(key_grads, 'ctx', scatter_dimension=0, tiled=True)  23.7 us
    all_gather x1, blocking collectives, on_device(): lax.all_gather(keys, 'ctx', axis=0, tiled=True)  14.8 us
    all_gather x1, blocking collectives, on_device(): lax.all_gather(values, 'ctx', axis=0, tiled=True)  14.4 us
    unnamed x10, local copies, waits for them, and re-layouts  5.18 us
    ppermute x1, starting transfers between devices, _reach_numbers(): u_next = lax.ppermute(u_next, net_axis, gallery)  5.05 us
    dot_general x1, matrix products, forward_update(): jnp.einsum('kgtr,rkd->kgtd', weights, value_heads, precision=lax.Precisio...  3.49 us
    cond x1, local copies, waits for them, and re-layouts, step(): return lax.cond(jnp.any(allowed), step_update, lambda state: state, carry)  2.55 us
    ppermute x2, starting transfers between devices, _reach_numbers(): val = lax.ppermute(val, net_axis, so_far_all)  2.5 us
  transfers between devices with their start and end apart: 4, of which 1 were waited for; matrix products, arithmetic and copies ran while one was open for 18% of the time, Pallas kernels for 0%

profile of v1, /device:TPU:0, one launch (start us, length us, event | category | flops | bytes accessed | tf_op | source)
XLA Modules:
  0.0 114.4 jit_solution(18164148165246017067)
XLA Ops:
  7.2 1.6 %copy.57 = bf16[128,256]{0,1:T(8,128)(2,1)} copy(bf16[128,256]{1,0:T(8,128)(2,1)} %param.11) | data formatting | bytes 131072 | tf_op args[1]
  8.8 5.0 %collective-permute-start.1 = (bf16[128,256]{0,1:T(8,128)(2,1)}, bf16[128,256]{0,1:T(8,128)(2,1)}, u32[]{:S(2)}, u32[]{:S(2)}) collective-permute-start(bf16[128,256]{0,1:T(8,128)(2,1)} %copy.57), channel_id=1, source_target_pairs={{0,12},{4,0},{8,4},{12,8},{1,13},{5,1},{9,5},{13,9},{2,14},{6,2},{... | collective-permute-start | bytes 196616 | tf_op jit(solution)/shard_map/ppermute | solution.py:28
  14.6 1.2 %dynamic_slice.12 = s32[1]{0:T(128)} dynamic-slice(s32[4]{0:T(128)} %param.14, s32[]{:T(128)S(6)} %select_n.76), dynamic_slice_sizes={1} | dynamic-slice | bytes 12 | tf_op jit(solution)/shard_map/dynamic_slice | solution.py:82
  16.9 0.8 and_reduce_fusion
  18.3 1.3 %copy.59 = bf16[128,2048]{0,1:T(8,128)(2,1)S(1)} copy(bf16[128,2048]{1,0:T(8,128)(2,1)} %param.10) | data formatting | bytes 1048576 | tf_op args[0]
  19.6 1.3 %copy.62 = bf16[128,2048]{0,1:T(8,128)(2,1)S(1)} copy(bf16[128,2048]{1,0:T(8,128)(2,1)} %param.13) | data formatting | bytes 1048576 | tf_op args[3]
  21.4 0.8 compare_and_fusion
  22.2 14.8 %all_gather.7 = bf16[512,256]{1,0:T(8,128)(2,1)} all-gather(bf16[128,256]{1,0:T(8,128)(2,1)S(1)} %copy-done.1), channel_id=1, replica_groups=mesh['grp'=2,'ctx'=4,'head'=4] {'ctx'}, dimensions={0}, use_global_device_ids=true | all-gather | bytes 327680 | tf_op jit(solution)/shard_map/all_gather | solution.py:179
  37.0 2.5 %collective-permute-start.2 = (bf16[128,256]{0,1:T(8,128)(2,1)}, bf16[128,256]{0,1:T(8,128)(2,1)}, u32[]{:S(2)}, u32[]{:S(2)}) collective-permute-start(bf16[128,256]{0,1:T(8,128)(2,1)} %collective-permute-done), channel_id=1, source_target_pairs={{0,4},{4,8},{8,12},{12,0},{1,5},{5,9},{9,13},{13,1},{2,6},{6,10},{... | collective-permute-start | bytes 196616 | tf_op jit(solution)/shard_map/ppermute | solution.py:25
  39.5 14.4 %all_gather.8 = bf16[512,256]{1,0:T(8,128)(2,1)S(1)} all-gather(bf16[128,256]{1,0:T(8,128)(2,1)S(1)} %copy-done.4), channel_id=1, replica_groups=mesh['grp'=2,'ctx'=4,'head'=4] {'ctx'}, dimensions={0}, use_global_device_ids=true | all-gather | bytes 327680 | tf_op jit(solution)/shard_map/all_gather | solution.py:194
  53.9 11.2 %conditional.2 = (f32[2,8,128]{2,1,0:T(8,128)}, f32[2,8,128]{2,1,0:T(8,128)S(1)}, f32[2,8,128,128]{3,2,1,0:T(8,128)S(1)}, f32[2,8,128]{2,1,0:T(8,128)}) conditional(s32[]{:T(128)} %convert_element_type.37, () %tuple.78, (pred[128,512]{0,1:T(8,128)(4,1)}, bf16[512,256]{1,0:T(8,128)(2,1)}, bf16[2,8,128,128]{2,3,1,0:T(8,128)(2,1)S(1)}, ...), branch_computations={%region_2.3_spmd, %region_3.6_spmd} | conditional | flops 1889804288 | bytes 17203260 | solution.py:118
  54.7 1.0 copy.60
  55.7 1.0 reshape.146
  56.7 1.0 select_reduce_fusion
  58.3 2.0 %fusion.1 = f32[2,8,128]{2,1,0:T(8,128)S(1)} fusion(f32[2,8,128,512]{3,2,1,0:T(8,128)S(1)} %get-tuple-element.545, f32[2,8,128]{2,1,0:T(8,128)} %get-tuple-element.554, pred[128,512]{1,0:T(8,128)(4,1)S(1)} %copy.60), kind=kLoop, calls=%fused_computation.3 | loop fusion | flops 4192256 | bytes 4276224 | tf_op jit(solution)/shard_map/cond/branch_1_fun/reduce_sum | solution.py:114
  60.3 3.5 %fusion.6 = f32[2,8,128,128]{3,2,1,0:T(8,128)S(1)} fusion(f32[2,8,128,512]{3,2,1,0:T(8,128)S(1)} %get-tuple-element.545, f32[2,8,128]{2,1,0:T(8,128)} %get-tuple-element.554, pred[128,512]{1,0:T(8,128)(4,1)S(1)} %copy.60, f32[2,8,128]{2,1,0:T(8,128)S(1)} %get-tuple-element.542, bf16[512,2,128,1]{2,1,0,3:T(2,128)(2,1)S(1)} %bitcast.79), kind=kOutput, calls=%fused_computation.8 | convolution fusion | flops 1614020608 | bytes 5586944 | tf_op jit(solution)/shard_map/cond/branch_1_fun/kgtr,rkd->kgtd/dot_general | solution.py:109
  63.8 1.3 %fusion.23 = (f32[2,8,128]{2,1,0:T(8,128)}, f32[2,8,128]{2,1,0:T(8,128)S(1)}) fusion(f32[2,8,128]{2,1,0:T(8,128)S(1)} %fusion.1, f32[2,8,128]{2,1,0:T(8,128)} %get-tuple-element.554), kind=kLoop, calls=%fused_computation.47 | loop fusion | flops 6144 | bytes 32768 | tf_op jit(solution)/shard_map/log | solution.py:185
  65.1 11.9 %conditional.3 = (f32[2,8,128,128]{3,2,1,0:T(8,128)}, f32[512,2,256]{0,2,1:T(8,128)}) conditional(s32[]{:T(128)} %convert_element_type.37, () %tuple.77, (pred[128,512]{0,1:T(8,128)(4,1)}, s32[]{:T(128)}, bf16[128,256]{1,0:T(8,128)(2,1)S(1)}, s32[]{:T(128)}, bf16[128,256]{0,1:T(8,128)(2,1)}, /*index=5*/s32[]{:T(128)}, ...), branch_computations={%region_6.7_spmd, %region_7.9_spmd.clone.clone} | conditional | flops 1353842688 | bytes 29983356 | solution.py:166
  65.2 1.2 %multiply_reduce_fusion = f32[2,8,128]{2,1,0:T(8,128)} fusion(f32[2,8,128,128]{3,2,1,0:T(8,128)S(1)} %get-tuple-element.517, f32[2,8,128,128]{3,2,1,0:T(8,128)S(1)} %get-tuple-element.516, f32[2,8,128]{2,1,0:T(8,128)S(1)} %get-tuple-element.515), kind=kLoop, calls=%fused_computation.25 | loop fusion | flops 784384 | bytes 2113536 | tf_op jit(solution)/shard_map/reduce_sum | solution.py:186
  67.4 0.9 constant_dynamic-update-slice_fusion.2
  68.3 0.9 constant_dynamic-update-slice_fusion.1
  69.2 0.9 constant_dynamic-update-slice_fusion
  70.8 1.0 fusion.14
  71.8 1.4 %multiply_convert_fusion = bf16[2,8,128,512]{2,3,1,0:T(8,128)(2,1)S(1)} fusion(f32[2,512,8,128]{3,1,2,0:T(8,128)S(1)} %fusion.25, bf16[2,8,128,128]{2,3,1,0:T(8,128)(2,1)S(1)} %get-tuple-element.514, f32[2,8,128]{2,1,0:T(8,128)S(1)} %copy-done.5, f32[2,8,128]{2,1,0:T(8,128)S(1)} %add.148, pred[128,512]{0,1:T(8,128)(4,1)S(1)} %copy-done.3, ...), kind=kOutput, calls=%fused_computation.18 | convolution fusion | flops 274726912 | bytes 7159808 | tf_op jit(solution)/shard_map/cond/branch_1_fun/kgtd,rkd->kgtr/dot_general | solution.py:132
  73.2 0.8 fusion.17
  74.0 2.0 %fusion.26 = f32[2,8,128,128]{3,2,1,0:T(8,128)} fusion(bf16[2,8,128,512]{2,3,1,0:T(8,128)(2,1)S(1)} %multiply_convert_fusion, bf16[512,2,128,1]{0,2,3,1:T(8,128)(2,1)S(1)} %bitcast.70), kind=kOutput, calls=%fused_computation.49 | convolution fusion | flops 268435456 | bytes 3407872 | tf_op jit(solution)/shard_map/cond/branch_1_fun/kgtr,rkd->kgtd/dot_general | solution.py:136
  75.9 1.1 pad_maximum_fusion
  77.0 2.5 %copy.66 = f32[512,2,256]{2,0,1:T(8,128)} copy(f32[512,2,256]{0,2,1:T(8,128)} %get-tuple-element.393) | data formatting | bytes 2097152 | tf_op jit(solution)/shard_map/cond | solution.py:166
  79.6 1.4 %fusion.21 = bf16[128,2,8,128]{3,0,2,1:T(8,128)(2,1)S(1)} fusion(f32[2,8,128,128]{3,2,1,0:T(8,128)} %get-tuple-element.392), kind=kLoop, calls=%fused_computation.34 | loop fusion | flops 524288 | bytes 1572864 | tf_op jit(solution)/shard_map/convert_element_type | solution.py:202
  81.3 0.9 copy.103
  82.2 23.7 %reduce-scatter.2.cloned.1.call-done = f32[128,2,256]{2,0,1:T(8,128)} async-done(((f32[512,2,256]{2,0,1:T(8,128)}), f32[128,2,256]{2,0,1:T(8,128)}) %reduce-scatter.2.cloned.1.call-update) | async-done | bytes 262160 | tf_op jit(solution)/shard_map/reduce_scatter | solution.py:197
  105.9 1.0 convert.4
  (36 shorter events, 5.7 us)
Async XLA Ops:
  7.2 9.3 %copy-start = (s32[4,2]{0,1:T(2,128)S(1)}, s32[4,2]{0,1:T(2,128)}, u32[]{:S(2)}) copy-start(s32[4,2]{0,1:T(2,128)} %param.15) | copy-start | bytes 100
  7.2 15.0 %copy-start.1 = (bf16[128,256]{1,0:T(8,128)(2,1)S(1)}, bf16[128,256]{1,0:T(8,128)(2,1)}, u32[]{:S(2)}) copy-start(bf16[128,256]{1,0:T(8,128)(2,1)} %param.11) | copy-start | bytes 196612
  7.2 32.3 %copy-start.4 = (bf16[128,256]{1,0:T(8,128)(2,1)S(1)}, bf16[128,256]{1,0:T(8,128)(2,1)}, u32[]{:S(2)}) copy-start(bf16[128,256]{1,0:T(8,128)(2,1)} %param.12) | copy-start | bytes 196612
  7.2 98.7 %reduce-scatter.2.cloned.1.call-start = ((), (), s32[]{:S(2)}) async-start(), calls=%async_computation.1 | async-start | bytes 1310720 | tf_op jit(solution)/shard_map/reduce_scatter | solution.py:197
  8.8 56.3 %collective-permute-start.1 = (bf16[128,256]{0,1:T(8,128)(2,1)}, bf16[128,256]{0,1:T(8,128)(2,1)}, u32[]{:S(2)}, u32[]{:S(2)}) collective-permute-start(bf16[128,256]{0,1:T(8,128)(2,1)} %copy.57), channel_id=1, source_target_pairs={{0,12},{4,0},{8,4},{12,8},{1,13},{5,1},{9,5},{13,9},{2,14},{6,2},{... | collective-permute-start | bytes 196616 | tf_op jit(solution)/shard_map/ppermute | solution.py:28
  13.9 23.1 %collective-permute-start = (bf16[128,256]{0,1:T(8,128)(2,1)}, bf16[128,256]{0,1:T(8,128)(2,1)}, u32[]{:S(2)}, u32[]{:S(2)}) collective-permute-start(bf16[128,256]{0,1:T(8,128)(2,1)} %copy.57), channel_id=1, source_target_pairs={{0,4},{4,8},{8,12},{12,0},{1,5},{5,9},{9,13},{13,1},{2,6},{6,10},{... | collective-permute-start | bytes 196616 | tf_op jit(solution)/shard_map/ppermute | solution.py:25
  37.0 28.1 %collective-permute-start.2 = (bf16[128,256]{0,1:T(8,128)(2,1)}, bf16[128,256]{0,1:T(8,128)(2,1)}, u32[]{:S(2)}, u32[]{:S(2)}) collective-permute-start(bf16[128,256]{0,1:T(8,128)(2,1)} %collective-permute-done), channel_id=1, source_target_pairs={{0,4},{4,8},{8,12},{12,0},{1,5},{5,9},{9,13},{13,1},{2,6},{6,10},{... | collective-permute-start | bytes 196616 | tf_op jit(solution)/shard_map/ppermute | solution.py:25
  56.7 3.6 %copy-start.2 = (bf16[512,2,128]{2,1,0:T(2,128)(2,1)S(1)}, bf16[512,2,128]{2,1,0:T(2,128)(2,1)}, u32[]{:S(2)}) copy-start(bf16[512,2,128]{2,1,0:T(2,128)(2,1)} %reshape.147) | copy-start | bytes 786436 | tf_op jit(solution)/shard_map/cond
  65.2 5.6 %copy-start.3 = (pred[128,512]{0,1:T(8,128)(4,1)S(1)}, pred[128,512]{0,1:T(8,128)(4,1)}, u32[]{:S(2)}) copy-start(pred[128,512]{0,1:T(8,128)(4,1)} %get-tuple-element.504) | copy-start | bytes 196612 | tf_op jit(solution)/shard_map/cond
  70.8 1.0 copy-start.5
Sparse Core Ops, SparseCore 0:
  79.7 26.1 reduce-scatter.1
